TPU v7x, 32 devices: a whole 2x2x4 slice. The times are simulated.
32 devices in a mesh: groups: 2 (over x), tm: 16 (over z, y, core).
Axes of the slice: x: 2, y: 2, z: 4, core: 2. Of those that a mesh axis runs over, the one named last changes fastest.
Arguments:
- state: float32 [32, 64, 1, 1440], P(('groups', 'tm')), parts along dimension 0, may hold values from -18 to 18
- observed: float32 [32, 64, 1, 1440], P(('groups', 'tm')), parts along dimension 0, may hold values from -6 to 6
- obs_mask: int32 [32, 64, 1, 1440], P(('groups', 'tm')), parts along dimension 0, may hold values 0 or 1
- noise: float32 [32, 64, 1, 1440], P(('groups', 'tm')), parts along dimension 0, may hold values from -6 to 6
- w_first: bfloat16 [256, 320, 3, 3], replicated, may hold values from -0.109375 to 0.109375
- b_first: float32 [256], replicated, may hold values from -3 to 3
- w_second: bfloat16 [64, 256, 3, 3], replicated, may hold values from -0.125 to 0.125
- b_second: float32 [64], replicated, may hold values from -3 to 3
Outputs:
- sample: float32 [32, 64, 1, 1440], P(('groups', 'tm')), parts along dimension 0
There are 2 independent parts, one for each index of `groups`. A program takes and returns all parts, laid end to end along the dimension named above; an argument that names none is the same for every part. Nothing has to cross between parts.
All inputs are finite; a program needn't handle non-finite values. No bound on the sum of `obs_mask` on one device may be relied on, other than what follows from the above.
Results may differ from a plain program's by a relative error of at most 0.00048.
Values may be sent and summed in bfloat16 or wider, within the bound.
No kernel may reach another device: no remote copies, remote signals or barrier semaphores. Data moves between devices by JAX's collectives and lax.ppermute only.
A program may use at most 64 MiB of HBM per device.

v0:
```python
import jax
import jax.numpy as jnp
from jax import lax
from jax.sharding import PartitionSpec as P


def shifted(value, axis, steps):
    count = lax.axis_size(axis)
    leading, last = (max(0, -steps), min(count, count - steps))
    return lax.ppermute(value, axis, [(source, source + steps) for source in range(leading, last)])


def conv_wrap(field, weights):
    wrapped = jnp.concatenate([field[..., -1:], field, field[..., :1]], axis=-1)
    padded = jnp.pad(wrapped, ((0, 0), (0, 0), (1, 1), (0, 0)))
    return lax.conv_general_dilated(
        padded,
        weights,
        (1, 1),
        "VALID",
        dimension_numbers=("NCHW", "OIHW", "NCHW"),
        preferred_element_type=jnp.float32,
    )


def first_layer(rounded, w_first):
    far_before = shifted(rounded, "tm", 2)
    near_before = shifted(rounded, "tm", 1)
    near_after = shifted(rounded, "tm", -1)
    far_after = shifted(rounded, "tm", -2)
    window = jnp.concatenate([far_before, near_before, rounded, near_after, far_after], axis=1)
    return conv_wrap(window, w_first)


def score(field, observed, mask_f, w_first, b_first, w_second, b_second):
    rounded = field.astype(jnp.bfloat16)
    pre = first_layer(rounded, w_first) + b_first[None, :, None, None]
    hidden = jax.nn.silu(pre).astype(jnp.bfloat16)
    out = conv_wrap(hidden, w_second) + b_second[None, :, None, None]
    return out + mask_f * (observed - field)


def on_device(state, observed, obs_mask, noise, w_first, b_first, w_second, b_second):
    mask_f = obs_mask.astype(jnp.float32)
    predicted = state + 0.5 * score(state, observed, mask_f, w_first, b_first, w_second, b_second)
    drift = score(predicted, observed, mask_f, w_first, b_first, w_second, b_second)
    zsq, gsq = lax.psum((jnp.sum(noise * noise), jnp.sum(drift * drift)), "tm")
    step = 2.0 * 0.16 * 0.16 * zsq / (gsq + 1e-06)
    return predicted + step * drift + jnp.sqrt(2.0 * step) * noise


def solution(mesh):
    return jax.shard_map(
        on_device,
        mesh=mesh,
        in_specs=(
            P(("groups", "tm"), None, None, None),
            P(("groups", "tm"), None, None, None),
            P(("groups", "tm"), None, None, None),
            P(("groups", "tm"), None, None, None),
            P(),
            P(),
            P(),
            P(),
        ),
        out_specs=P(("groups", "tm"), None, None, None),
        check_vma=False,
    )
```

profile of v0, /device:TPU:0, one launch (start us, length us, event | category | flops | bytes accessed | tf_op | source)
XLA Modules:
  0.0 157.0 jit_solution(615614785014657253)
XLA Ops:
  0.0 1.4 convert_element_type.21
  1.4 4.9 %collective-permute-start = (bf16[1,64,1,1440]{3,2,1,0:T(2,128)(2,1)S(1)}, bf16[1,64,1,1440]{3,2,1,0:T(2,128)(2,1)S(1)}, u32[]{:S(2)}, u32[]{:S(2)}) collective-permute-start(bf16[1,64,1,1440]{3,2,1,0:T(2,128)(2,1)S(1)} %convert_element_type.21), channel_id=1, source_target_pairs={{0,2},{1,3},{2,4},{3,5},{4,6},{5,7},{6,8},{7,9},{8,10},{9,11},{10,... | collective-permute-start | bytes 552968 | tf_op jit(solution)/shard_map/ppermute | solution.py:10
  6.3 1.5 collective-permute-start.1
  7.8 1.3 collective-permute-start.2
  9.1 1.3 collective-permute-start.3
  10.4 18.0 %collective-permute-done = bf16[1,64,1,1440]{3,2,1,0:T(2,128)(2,1)S(1)} collective-permute-done((bf16[1,64,1,1440]{3,2,1,0:T(2,128)(2,1)S(1)}, bf16[1,64,1,1440]{3,2,1,0:T(2,128)(2,1)S(1)}, u32[]{:S(2)}, u32[]{:S(2)}) %collective-permute-start) | collective-permute-done | bytes 184352 | tf_op jit(solution)/shard_map/ppermute | solution.py:10
  28.4 0.4 constant_dynamic-update-slice_fusion.4
  28.9 0.4 constant_dynamic-update-slice_fusion.3
  29.3 0.3 constant_dynamic-update-slice_fusion.2
  29.6 0.4 constant_dynamic-update-slice_fusion.1
  30.1 0.4 constant_dynamic-update-slice_fusion
  30.6 1.3 fusion.53
  31.9 13.1 %concatenate.19 = bf16[1,320,1,1442]{3,2,1,0:T(2,128)(2,1)S(1)} concatenate(bf16[1,320,1,1]{3,2,1,0:T(2,128)(2,1)} %get-tuple-element.10, bf16[1,320,1,1440]{3,2,1,0:T(2,128)(2,1)} %copy-done.1, bf16[1,320,1,1]{3,2,1,0:T(2,128)(2,1)} %get-tuple-element.9), dimensions={3} | concatenate | bytes 1845760 | tf_op jit(solution)/shard_map/concatenate | solution.py:14
  45.0 0.1 copy.82
  45.2 1.0 pad.6
  46.2 3.3 %reshape.50 = bf16[320,1,1,8,181]{4,3,0,2,1:T(8,128)(2,1)S(1)} reshape(bf16[320,1,1,1448]{3,0,2,1:T(8,128)(2,1)} %pad.6) | data formatting | bytes 1853440 | tf_op jit(solution)/shard_map/conv_general_dilated | solution.py:16
  49.5 2.1 %copy.33 = bf16[320,1,1,8,181]{0,3,4,2,1:T(8,128)(2,1)} copy(bf16[320,1,1,8,181]{4,3,0,2,1:T(8,128)(2,1)S(1)} %reshape.50) | data formatting | bytes 1853440 | tf_op jit(solution)/shard_map/conv_general_dilated | solution.py:16
  51.6 0.7 slice.42
  52.3 4.0 %multiply_convert_fusion.1 = bf16[1,8,181,256]{3,1,2,0:T(8,128)(2,1)S(1)} fusion(bf16[256,320,3,3]{0,1,3,2:T(8,128)(2,1)S(1)} %copy-done, bf16[320,1,1,7,2]{0,3,4,2,1:T(8,128)(2,1)S(1)} %slice.42, bf16[320,1,1,8,181]{0,3,4,2,1:T(8,128)(2,1)} %copy.33, f32[256]{0:T(256)S(1)} %copy-done.14, pred[8,181]{0,1:T(8,128)(4,1)S(1)} %copy-done.15), kind=kOutput, calls=%fused_computation.7 | convolution fusion | flops 717126656 | bytes 3154088 | tf_op jit(solution)/shard_map/conv_general_dilated | solution.py:16
  56.4 0.1 copy.34
  56.5 1.1 reshape.12
  57.6 1.2 slice_bitcast_fusion.1
  58.8 2.8 %concatenate.20 = bf16[1,256,1,1442]{1,3,0,2:T(8,128)(2,1)S(1)} concatenate(bf16[1,256,1,1]{1,3,0,2:T(2,128)(2,1)S(1)} %get-tuple-element.16, bf16[1,256,1,1440]{1,3,0,2:T(8,128)(2,1)S(1)} %slice_bitcast_fusion.1, bf16[1,256,1,1]{1,3,0,2:T(2,128)(2,1)S(1)} %get-tuple-element.15), dimensions={3} | concatenate | bytes 1476608 | tf_op jit(solution)/shard_map/concatenate | solution.py:14
  61.7 0.2 reshape.15
  61.9 0.1 copy.36
  62.1 0.6 copy-done.13
  62.6 1.9 %fusion.18 = f32[1,8,181,64]{3,1,2,0:T(8,128)S(1)} fusion(bf16[64,256,3,3]{1,0,3,2:T(8,128)(2,1)S(1)} %copy-done.13, bf16[256,1,1,7,2]{0,3,4,2,1:T(8,128)(2,1)S(1)} %slice.46, bf16[256,1,1,8,181]{0,3,4,2,1:T(8,128)(2,1)S(1)} %copy.36), kind=kOutput, calls=%fused_computation.21 | convolution fusion | flops 144592896 | bytes 1414144 | tf_op jit(solution)/shard_map/conv_general_dilated | solution.py:16
  64.5 0.4 copy.37
  64.9 0.1 select_add_fusion.1
  65.0 0.3 copy.38
  65.3 1.0 reshape.31
  66.3 1.9 %fusion.51 = (bf16[1,64,1,1440]{3,1,0,2:T(8,128)(2,1)S(1)}, f32[1,64,1,1440]{3,1,0,2:T(8,128)}) fusion(f32[1,64,1,1440]{3,2,1,0:T(1,128)S(1)} %copy-done.4, s32[1,64,1,1440]{3,2,1,0:T(1,128)S(1)} %copy-done.5, f32[1,1,1448,64]{2,3,1,0:T(8,128)} %reshape.31, f32[1,64,1,1440]{3,2,1,0:T(1,128)S(1)} %copy-done.3), kind=kLoop, calls=%fused_computation.72 | loop fusion | flops 645120 | bytes 2027520 | tf_op jit(solution)/shard_map/convert_element_type | solution.py:36
  68.2 7.2 %collective-permute-start.4 = (bf16[1,64,1,1440]{3,1,0,2:T(8,128)(2,1)S(1)}, bf16[1,64,1,1440]{3,1,0,2:T(8,128)(2,1)S(1)}, u32[]{:S(2)}, u32[]{:S(2)}) collective-permute-start(bf16[1,64,1,1440]{3,1,0,2:T(8,128)(2,1)S(1)} %get-tuple-element.7), channel_id=1, source_target_pairs={{0,2},{1,3},{2,4},{3,5},{4,6},{5,7},{6,8},{7,9},{8,10},{9,11},{10,... | collective-permute-start | bytes 552968 | tf_op jit(solution)/shard_map/ppermute | solution.py:10
  75.5 1.4 multiply_reduce_fusion.1
  76.9 1.3 collective-permute-start.5
  78.2 1.3 collective-permute-start.6
  79.5 1.3 collective-permute-start.7
  80.9 2.0 %collective-permute-done.6 = bf16[1,64,1,1440]{3,1,0,2:T(8,128)(2,1)S(1)} collective-permute-done((bf16[1,64,1,1440]{3,1,0,2:T(8,128)(2,1)S(1)}, bf16[1,64,1,1440]{3,1,0,2:T(8,128)(2,1)S(1)}, u32[]{:S(2)}, u32[]{:S(2)}) %collective-permute-start.6) | collective-permute-done | bytes 184352 | tf_op jit(solution)/shard_map/ppermute | solution.py:10
  82.9 8.5 %collective-permute-done.7 = bf16[1,64,1,1440]{3,1,0,2:T(8,128)(2,1)S(1)} collective-permute-done((bf16[1,64,1,1440]{3,1,0,2:T(8,128)(2,1)S(1)}, bf16[1,64,1,1440]{3,1,0,2:T(8,128)(2,1)S(1)}, u32[]{:S(2)}, u32[]{:S(2)}) %collective-permute-start.7) | collective-permute-done | bytes 184352 | tf_op jit(solution)/shard_map/ppermute | solution.py:10
  91.5 0.1 fusion.54
  91.6 0.9 copy-done.9
  92.5 2.6 %concatenate.22 = bf16[1,320,1,1442]{3,1,0,2:T(8,128)(2,1)S(1)} concatenate(bf16[1,320,1,1]{3,1,0,2:T(8,128)(2,1)S(1)} %get-tuple-element.12, bf16[1,320,1,1440]{3,1,0,2:T(8,128)(2,1)} %copy-done.9, bf16[1,320,1,1]{3,1,0,2:T(8,128)(2,1)S(1)} %get-tuple-element.11), dimensions={3} | concatenate | bytes 1845760 | tf_op jit(solution)/shard_map/concatenate | solution.py:14
  95.1 1.0 pad.10
  96.1 3.3 %reshape.51 = bf16[320,1,1,8,181]{4,3,0,2,1:T(8,128)(2,1)S(1)} reshape(bf16[320,1,1,1448]{3,0,2,1:T(8,128)(2,1)} %pad.10) | data formatting | bytes 1853440 | tf_op jit(solution)/shard_map/conv_general_dilated | solution.py:16
  99.4 2.1 %copy.45 = bf16[320,1,1,8,181]{0,3,4,2,1:T(8,128)(2,1)} copy(bf16[320,1,1,8,181]{4,3,0,2,1:T(8,128)(2,1)S(1)} %reshape.51) | data formatting | bytes 1853440 | tf_op jit(solution)/shard_map/conv_general_dilated | solution.py:16
  101.5 0.7 slice.50
  102.2 4.0 %multiply_convert_fusion = bf16[1,8,181,256]{3,1,2,0:T(8,128)(2,1)S(1)} fusion(bf16[256,320,3,3]{0,1,3,2:T(8,128)(2,1)S(1)} %copy-done, bf16[320,1,1,7,2]{0,3,4,2,1:T(8,128)(2,1)S(1)} %slice.50, bf16[320,1,1,8,181]{0,3,4,2,1:T(8,128)(2,1)} %copy.45, f32[256]{0:T(256)S(1)} %copy-done.14, pred[8,181]{0,1:T(8,128)(4,1)S(1)} %copy-done.15), kind=kOutput, calls=%fused_computation.6 | convolution fusion | flops 717126656 | bytes 3154088 | tf_op jit(solution)/shard_map/conv_general_dilated | solution.py:16
  106.3 0.1 copy.46
  106.4 1.1 reshape.24
  107.5 1.2 slice_bitcast_fusion
  108.7 0.9 copy-done.8
  109.6 3.8 %concatenate.23 = bf16[1,256,1,1442]{1,3,0,2:T(8,128)(2,1)S(1)} concatenate(bf16[1,256,1,1]{1,3,0,2:T(2,128)(2,1)S(1)} %get-tuple-element.14, bf16[1,256,1,1440]{1,3,0,2:T(8,128)(2,1)} %copy-done.8, bf16[1,256,1,1]{1,3,0,2:T(2,128)(2,1)S(1)} %get-tuple-element.13), dimensions={3} | concatenate | bytes 1476608 | tf_op jit(solution)/shard_map/concatenate | solution.py:14
  113.4 0.9 pad.12
  114.3 1.3 reshape.27
  115.6 0.1 copy.48
  115.8 1.9 %fusion.22 = f32[1,8,181,64]{3,1,2,0:T(8,128)S(1)} fusion(bf16[64,256,3,3]{1,0,3,2:T(8,128)(2,1)S(1)} %copy-done.13, bf16[256,1,1,7,2]{0,3,4,2,1:T(8,128)(2,1)S(1)} %slice.54, bf16[256,1,1,8,181]{0,3,4,2,1:T(8,128)(2,1)S(1)} %copy.48), kind=kOutput, calls=%fused_computation.24 | convolution fusion | flops 144592896 | bytes 1414144 | tf_op jit(solution)/shard_map/conv_general_dilated | solution.py:16
  117.7 1.2 copy.49
  118.9 1.2 select_add_fusion
  120.1 1.1 copy.50
  121.2 1.3 reshape.33
  122.5 0.7 multiply_reduce_fusion
  123.2 30.1 %all-reduce = (f32[]{:T(128)}, f32[]{:T(128)}) all-reduce(f32[]{:T(128)} %multiply_reduce_fusion.1, f32[]{:T(128)} %multiply_reduce_fusion), channel_id=1, replica_groups=mesh['groups'=2,'tm'=16] {'tm'}, use_global_device_ids=true, to_apply=%region_1.2 | all-reduce | flops 2 | bytes 16 | tf_op jit(solution)/shard_map/psum | solution.py:47
  154.7 1.1 fusion.36
  155.8 1.2 copy.53
  (44 shorter events, 0.2 us)
Async XLA Ops:
  0.0 52.3 %copy-start = (bf16[256,320,3,3]{0,1,3,2:T(8,128)(2,1)S(1)}, bf16[256,320,3,3]{0,1,3,2:T(8,128)(2,1)}, u32[]{:S(2)}) copy-start(bf16[256,320,3,3]{0,1,3,2:T(8,128)(2,1)} %param.12) | copy-start | bytes 4423684
  0.0 29.3 %copy-start.2 = (f32[1,64,1,1440]{3,2,1,0:T(1,128)S(1)}, f32[1,64,1,1440]{3,2,1,0:T(1,128)}, u32[]{:S(2)}) copy-start(f32[1,64,1,1440]{3,2,1,0:T(1,128)} %param.8) | copy-start | bytes 1105924
  1.4 27.0 %collective-permute-start = (bf16[1,64,1,1440]{3,2,1,0:T(2,128)(2,1)S(1)}, bf16[1,64,1,1440]{3,2,1,0:T(2,128)(2,1)S(1)}, u32[]{:S(2)}, u32[]{:S(2)}) collective-permute-start(bf16[1,64,1,1440]{3,2,1,0:T(2,128)(2,1)S(1)} %convert_element_type.21), channel_id=1, source_target_pairs={{0,2},{1,3},{2,4},{3,5},{4,6},{5,7},{6,8},{7,9},{8,10},{9,11},{10,... | collective-permute-start | bytes 552968 | tf_op jit(solution)/shard_map/ppermute | solution.py:10
  6.3 22.5 %collective-permute-start.1 = (bf16[1,64,1,1440]{3,2,1,0:T(2,128)(2,1)S(1)}, bf16[1,64,1,1440]{3,2,1,0:T(2,128)(2,1)S(1)}, u32[]{:S(2)}, u32[]{:S(2)}) collective-permute-start(bf16[1,64,1,1440]{3,2,1,0:T(2,128)(2,1)S(1)} %convert_element_type.21), channel_id=1, source_target_pairs={{0,1},{1,2},{2,3},{3,4},{4,5},{5,6},{6,7},{7,8},{8,9},{9,10},{10,1... | collective-permute-start | bytes 552968 | tf_op jit(solution)/shard_map/ppermute | solution.py:10
  7.8 21.8 %collective-permute-start.2 = (bf16[1,64,1,1440]{3,2,1,0:T(2,128)(2,1)S(1)}, bf16[1,64,1,1440]{3,2,1,0:T(2,128)(2,1)S(1)}, u32[]{:S(2)}, u32[]{:S(2)}) collective-permute-start(bf16[1,64,1,1440]{3,2,1,0:T(2,128)(2,1)S(1)} %convert_element_type.21), channel_id=1, source_target_pairs={{1,0},{2,1},{3,2},{4,3},{5,4},{6,5},{7,6},{8,7},{9,8},{10,9},{11,1... | collective-permute-start | bytes 552968 | tf_op jit(solution)/shard_map/ppermute | solution.py:10
  9.1 21.0 %collective-permute-start.3 = (bf16[1,64,1,1440]{3,2,1,0:T(2,128)(2,1)S(1)}, bf16[1,64,1,1440]{3,2,1,0:T(2,128)(2,1)S(1)}, u32[]{:S(2)}, u32[]{:S(2)}) collective-permute-start(bf16[1,64,1,1440]{3,2,1,0:T(2,128)(2,1)S(1)} %convert_element_type.21), channel_id=1, source_target_pairs={{2,0},{3,1},{4,2},{5,3},{6,4},{7,5},{8,6},{9,7},{10,8},{11,9},{12,... | collective-permute-start | bytes 552968 | tf_op jit(solution)/shard_map/ppermute | solution.py:10
  30.6 1.4 copy-start.1
  49.5 2.9 %copy-start.14 = (f32[256]{0:T(256)S(1)}, f32[256]{0:T(256)}, u32[]{:S(2)}) copy-start(f32[256]{0:T(256)} %param.13) | copy-start | bytes 3076
  49.5 2.8 %copy-start.15 = (pred[8,181]{0,1:T(8,128)(4,1)S(1)}, pred[8,181]{0,1:T(8,128)(4,1)}, u32[]{:S(2)}) copy-start(pred[8,181]{0,1:T(8,128)(4,1)} %constant.40) | copy-start | bytes 4348
  61.7 1.0 copy-start.13
  62.6 2.2 %copy-start.11 = (pred[8,181]{1,0:T(8,128)(4,1)S(1)}, pred[8,181]{1,0:T(8,128)(4,1)}, u32[]{:S(2)}) copy-start(pred[8,181]{1,0:T(8,128)(4,1)} %constant.36) | copy-start | bytes 4348
  62.6 2.3 %copy-start.12 = (f32[64]{0:T(128)S(1)}, f32[64]{0:T(128)}, u32[]{:S(2)}) copy-start(f32[64]{0:T(128)} %param.15) | copy-start | bytes 772
  64.9 1.4 copy-start.3
  64.9 1.4 copy-start.4
  64.9 1.4 copy-start.5
  66.3 9.1 %copy-start.10 = (f32[1,64,1,1440]{3,2,1,0:T(1,128)S(1)}, f32[1,64,1,1440]{3,2,1,0:T(1,128)}, u32[]{:S(2)}) copy-start(f32[1,64,1,1440]{3,2,1,0:T(1,128)} %param.11) | copy-start | bytes 1105924
  68.2 12.6 %collective-permute-start.4 = (bf16[1,64,1,1440]{3,1,0,2:T(8,128)(2,1)S(1)}, bf16[1,64,1,1440]{3,1,0,2:T(8,128)(2,1)S(1)}, u32[]{:S(2)}, u32[]{:S(2)}) collective-permute-start(bf16[1,64,1,1440]{3,1,0,2:T(8,128)(2,1)S(1)} %get-tuple-element.7), channel_id=1, source_target_pairs={{0,2},{1,3},{2,4},{3,5},{4,6},{5,7},{6,8},{7,9},{8,10},{9,11},{10,... | collective-permute-start | bytes 552968 | tf_op jit(solution)/shard_map/ppermute | solution.py:10
  76.9 3.9 %collective-permute-start.5 = (bf16[1,64,1,1440]{3,1,0,2:T(8,128)(2,1)S(1)}, bf16[1,64,1,1440]{3,1,0,2:T(8,128)(2,1)S(1)}, u32[]{:S(2)}, u32[]{:S(2)}) collective-permute-start(bf16[1,64,1,1440]{3,1,0,2:T(8,128)(2,1)S(1)} %get-tuple-element.7), channel_id=1, source_target_pairs={{0,1},{1,2},{2,3},{3,4},{4,5},{5,6},{6,7},{7,8},{8,9},{9,10},{10,1... | collective-permute-start | bytes 552968 | tf_op jit(solution)/shard_map/ppermute | solution.py:10
  78.2 4.7 %collective-permute-start.6 = (bf16[1,64,1,1440]{3,1,0,2:T(8,128)(2,1)S(1)}, bf16[1,64,1,1440]{3,1,0,2:T(8,128)(2,1)S(1)}, u32[]{:S(2)}, u32[]{:S(2)}) collective-permute-start(bf16[1,64,1,1440]{3,1,0,2:T(8,128)(2,1)S(1)} %get-tuple-element.7), channel_id=1, source_target_pairs={{1,0},{2,1},{3,2},{4,3},{5,4},{6,5},{7,6},{8,7},{9,8},{10,9},{11,1... | collective-permute-start | bytes 552968 | tf_op jit(solution)/shard_map/ppermute | solution.py:10
  79.5 12.0 %collective-permute-start.7 = (bf16[1,64,1,1440]{3,1,0,2:T(8,128)(2,1)S(1)}, bf16[1,64,1,1440]{3,1,0,2:T(8,128)(2,1)S(1)}, u32[]{:S(2)}, u32[]{:S(2)}) collective-permute-start(bf16[1,64,1,1440]{3,1,0,2:T(8,128)(2,1)S(1)} %get-tuple-element.7), channel_id=1, source_target_pairs={{2,0},{3,1},{4,2},{5,3},{6,4},{7,5},{8,6},{9,7},{10,8},{11,9},{12,... | collective-permute-start | bytes 552968 | tf_op jit(solution)/shard_map/ppermute | solution.py:10
  91.5 1.0 copy-start.9
  108.7 0.9 copy-start.8
  118.9 3.6 %copy-start.6 = (s32[1,64,1,1440]{3,2,1,0:T(1,128)S(1)}, s32[1,64,1,1440]{3,2,1,0:T(1,128)}, u32[]{:S(2)}) copy-start(s32[1,64,1,1440]{3,2,1,0:T(1,128)} %param.10) | copy-start | bytes 1105924
  118.9 3.6 %copy-start.7 = (f32[1,64,1,1440]{3,1,0,2:T(8,128)S(1)}, f32[1,64,1,1440]{3,1,0,2:T(8,128)}, u32[]{:S(2)}) copy-start(f32[1,64,1,1440]{3,1,0,2:T(8,128)} %get-tuple-element.8) | copy-start | bytes 1105924
where the time goes:
time: 158 us; the launch traced here: 157 us
  local copies, waits for them, and re-layouts  56.3 us (36%)
  blocking collectives  30.1 us (19%)
  waiting for transfers between devices  28.6 us (18%)
  starting transfers between devices  20.1 us (13%)
  matrix products  11.8 us (7%)
  other arithmetic  8.22 us (5%)
  between operations  1.86 us (1%)
    psum x1, blocking collectives, on_device(): zsq, gsq = lax.psum((jnp.sum(noise * noise), jnp.sum(drift * drift)), 'tm')  30.1 us
    ppermute x8, waiting for transfers between devices, shifted(): lax.ppermute(value, axis, [(source, source + steps) for source in range(l...  28.6 us
    concatenate x8, local copies, waits for them, and re-layouts, conv_wrap(): wrapped = jnp.concatenate([field[..., -1:], field, field[..., :1]], axis=-1)  25.4 us
    ppermute x8, starting transfers between devices, shifted(): lax.ppermute(value, axis, [(source, source + steps) for source in range(l...  20.1 us
    conv_general_dilated x14, local copies, waits for them, and re-layouts, conv_wrap(): lax.conv_general_dilated(padded, weights, (1, 1), 'VALID', dimension_numb...  15.6 us
    conv_general_dilated x4, matrix products, conv_wrap(): lax.conv_general_dilated(padded, weights, (1, 1), 'VALID', dimension_numb...  11.8 us
    convert_element_type x6, local copies, waits for them, and re-layouts, score(): hidden = jax.nn.silu(pre).astype(jnp.bfloat16)  4.83 us
    unnamed x40, local copies, waits for them, and re-layouts  3.81 us
  transfers between devices with their start and end apart: 8, of which 3 were waited for; matrix products, arithmetic and copies ran while one was open for 2% of the time, Pallas kernels for 0%

commit v1 on v0

v1 whole, which is shorter than its diff:
```python
import functools

import jax
import jax.numpy as jnp
from jax import lax
from jax.experimental import pallas as pl
from jax.experimental.pallas import tpu as pltpu
from jax.sharding import PartitionSpec as P

LANES = 128
TILE = 256
VMEM = pl.BlockSpec(memory_space=pltpu.VMEM)
SMEM = pl.BlockSpec(memory_space=pltpu.SMEM)


def call(body, outs, scratch=(), cost=(0, 0)):
    return pl.pallas_call(
        body,
        out_shape=outs,
        out_specs=jax.tree.map(lambda _: VMEM, outs),
        scratch_shapes=list(scratch),
        cost_estimate=pl.CostEstimate(flops=cost[0], bytes_accessed=cost[1], transcendentals=0),
        compiler_params=pltpu.CompilerParams(vmem_limit_bytes=24 << 20),
    )


def wrap(value, lon):
    width = value.shape[1]
    rest = lon % LANES
    first, last = value[:, :LANES], value[:, width - LANES :]
    lane = lax.broadcasted_iota(jnp.int32, last.shape, 1)
    ahead = pltpu.roll(first, rest, 1)
    behind = pltpu.roll(last, LANES - rest, 1)
    tail = jnp.where(lane < rest, last, jnp.where(lane < rest + 2, ahead, behind))
    return jnp.concatenate([value[:, : width - LANES], tail], axis=1)


def widened(value, width):
    rows, lon = value.shape
    return jnp.concatenate([value, jnp.zeros((rows, width - lon), value.dtype)], axis=1)


def cast_body(state_ref, out_ref):
    lon = state_ref.shape[-1]
    out_ref[...] = wrap(widened(state_ref[0, :, 0, :], out_ref.shape[1]), lon).astype(jnp.bfloat16)


def prepare_body(odd_ref, state_ref, seen_ref, mask_ref, noise_ref, w_ref, bias_ref, start_ref, zsq_ref, weights_ref):
    width = start_ref.shape[1]
    state, seen = state_ref[0, :, 0, :], seen_ref[0, :, 0, :]
    mask = mask_ref[0, :, 0, :].astype(jnp.float32)
    start_ref[...] = widened(state + 0.5 * (mask * (seen - state) + bias_ref[...]), width)
    noise = noise_ref[0, :, 0, :]
    zsq_ref[...] = jnp.full(zsq_ref.shape, jnp.sum(noise * noise))
    taps, window, hidden = w_ref.shape[1:]
    rows = state.shape[0]
    hours = window // rows
    for tap in range(taps):
        for slot in range(hours):
            source = jnp.where(odd_ref[0] == 1, hours - 1 - slot, slot)
            block = w_ref[0, tap, pl.ds(pl.multiple_of(source * rows, rows), rows), :]
            at = (tap * hours + slot) * rows
            weights_ref[:, at : at + rows] = block.T


def convolved(field_refs, weights_ref, bias_ref, second_ref, stack, side):
    rows, width = field_refs[0].shape
    hours = len(field_refs)
    for slot, ref in enumerate(field_refs):
        value = ref[...]
        for tap in range(3):
            at = (tap * hours + slot) * rows
            moved = value if tap == 1 else pltpu.roll(value, 1 if tap == 0 else width - 1, 1)
            stack[at : at + rows, :] = moved
    weights, second = weights_ref[...], second_ref[0].reshape(-1, second_ref.shape[-1])
    bias = bias_ref[...]
    for n in range(0, width, TILE):
        pre = jnp.dot(weights, stack[:, n : n + TILE], preferred_element_type=jnp.float32) + bias
        half = 0.5 * pre
        hidden = (half + half * jnp.tanh(half)).astype(jnp.bfloat16)
        side[:, n : n + TILE] = jnp.dot(second, hidden, preferred_element_type=jnp.float32)
    return side[rows : 2 * rows] + pltpu.roll(side[:rows], 1, 1) + pltpu.roll(side[2 * rows :], width - 1, 1)


def first_body(lon, *refs):
    fields, (weights, bias, second, start, out_ref, rounded_ref, stack, side) = refs[:5], refs[5:]
    predicted = start[...] + 0.5 * convolved(fields, weights, bias, second, stack, side)
    out_ref[...] = predicted
    rounded_ref[...] = wrap(predicted, lon).astype(jnp.bfloat16)


def second_body(lon, *refs):
    fields, rest = refs[:5], refs[5:]
    weights, bias, second, bias_two, predicted, seen_ref, mask_ref, out_ref, gsq_ref, stack, side = rest
    conv = convolved(fields, weights, bias, second, stack, side)[:, :lon]
    mask = mask_ref[0, :, 0, :].astype(jnp.float32)
    drift = conv + bias_two[...] + mask * (seen_ref[0, :, 0, :] - predicted[:, :lon])
    out_ref[...] = drift
    gsq_ref[...] = jnp.full(gsq_ref.shape, jnp.sum(drift * drift))


def last_body(sums_ref, predicted, drift, noise_ref, out_ref):
    lon = out_ref.shape[-1]
    scale = 2.0 * 0.16 * 0.16 * sums_ref[0, 0] / (sums_ref[1, 0] + 1e-06)
    step = jnp.full((1, LANES), scale)
    root = jnp.sqrt(2.0 * step)[:, :1]
    out_ref[0, :, 0, :] = predicted[:, :lon] + step[:, :1] * drift[...] + root * noise_ref[0, :, 0, :]


def exchange(field, count):
    near = [(d, d + 1) for d in range(1, count - 1, 2)] + [(d, d - 1) for d in range(2, count, 2)]
    far = [(d, d + 2) for d in range(0, count - 2, 2)] + [(d, d - 2) for d in range(3, count, 2)]
    swap = [(d, d ^ 1) for d in range(count)]
    one = lax.ppermute(field, "tm", near)
    two = lax.ppermute(field, "tm", far)
    beside = lax.ppermute(field, "tm", swap)
    passed = lax.ppermute(one, "tm", swap)
    return two, one, field, beside, passed


def summed(value, count):
    distance = 1
    while distance < count:
        value = value + lax.ppermute(value, "tm", [(d, d ^ distance) for d in range(count)])
        distance *= 2
    return value


def on_device(state, observed, obs_mask, noise, w_first, b_first, w_second, b_second):
    count = lax.axis_size("tm")
    _, rows, _, lon = state.shape
    hid = b_first.shape[0]
    width = -(-(lon + 4) // TILE) * TILE
    window = w_first.shape[1]
    f32, bf16 = jnp.float32, jnp.bfloat16
    w_one = w_first.transpose(2, 3, 1, 0)[1:2]
    w_two = w_second.transpose(2, 3, 0, 1)[1]
    bias_one, bias_two = b_first[:, None], b_second[:, None]
    odd = (lax.axis_index("tm") % 2).astype(jnp.int32).reshape(1)
    shape = jax.ShapeDtypeStruct
    field, small = shape((rows, width), bf16), shape((1, LANES), f32)

    rounded = call(cast_body, field)(state)
    start, zsq, weights = pl.pallas_call(
        prepare_body,
        in_specs=[SMEM] + [VMEM] * 6,
        out_specs=[VMEM] * 3,
        out_shape=[shape((rows, width), f32), small, shape((hid, 3 * window), bf16)],
        compiler_params=pltpu.CompilerParams(vmem_limit_bytes=24 << 20),
    )(odd, state, observed, obs_mask, noise, w_one, bias_two)
    scratch = (pltpu.VMEM((3 * window, width), bf16), pltpu.VMEM((3 * rows, width), f32))
    predicted, rounded = call(functools.partial(first_body, lon), [shape((rows, width), f32), field], scratch)(
        *exchange(rounded, count), weights, bias_one, w_two[None], start
    )
    drift, gsq = call(functools.partial(second_body, lon), [shape((rows, lon), f32), small], scratch)(
        *exchange(rounded, count), weights, bias_one, w_two[None], bias_two, predicted, observed, obs_mask
    )
    sums = summed(jnp.concatenate([zsq, gsq]), count)
    return pl.pallas_call(
        last_body,
        in_specs=[SMEM] + [VMEM] * 3,
        out_specs=VMEM,
        out_shape=shape(state.shape, f32),
        compiler_params=pltpu.CompilerParams(vmem_limit_bytes=24 << 20),
    )(sums, predicted, drift, noise)


def solution(mesh):
    return jax.shard_map(
        on_device,
        mesh=mesh,
        in_specs=(
            P(("groups", "tm"), None, None, None),
            P(("groups", "tm"), None, None, None),
            P(("groups", "tm"), None, None, None),
            P(("groups", "tm"), None, None, None),
            P(),
            P(),
            P(),
            P(),
        ),
        out_specs=P(("groups", "tm"), None, None, None),
        check_vma=False,
    )
```

time: 158 us -> 53.9 us (0.34)
  local copies, waits for them, and re-layouts: 56.3 us -> 4.52 us
  blocking collectives: 30.1 us -> 0 us
  waiting for transfers between devices: 28.6 us -> 10.8 us
  matrix products: 11.8 us -> 0 us
  starting transfers between devices: 20.1 us -> 29.2 us
  Pallas kernels: 0 us -> 8.81 us
  other arithmetic: 8.22 us -> 0.03 us
  between operations: 1.86 us -> 0.17 us
    psum x1 -> x0, blocking collectives: 30.1 us -> none  [on_device(): zsq, gsq = lax.psum((jnp.sum(noise * noise), jnp.sum(drift * drift)), 'tm')]
    concatenate x10 -> x0, local copies, waits for them, and re-layouts: 25.9 us -> none  [the longest x8 25.4 us: conv_wrap(): wrapped = jnp.concatenate([field[..., -1:], field, field[..., :1]], axis=-1)]
    ppermute x8 -> x12, waiting for transfers between devices: 28.6 us -> 10.8 us  [the longest x4 5.81 us: summed(): lax.ppermute(value, 'tm', [(d, d ^ distance) for d in range(count)])]
    conv_general_dilated x14 -> x0, local copies, waits for them, and re-layouts: 15.6 us -> none  [conv_wrap(): lax.conv_general_dilated(padded, weights, (1, 1), 'VALID', dimension_numb...]
    conv_general_dilated x4 -> x0, matrix products: 11.8 us -> none  [conv_wrap(): lax.conv_general_dilated(padded, weights, (1, 1), 'VALID', dimension_numb...]
    ppermute x8 -> x12, starting transfers between devices: 20.1 us -> 29.2 us  [the longest x2 10.3 us: exchange(): beside = lax.ppermute(field, 'tm', swap)]
    pallas_call x0 -> x5, Pallas kernels: none -> 8.81 us  [the longest x1 3.23 us: on_device(): call(functools.partial(second_body, lon), [shape((rows, lon), f32), small...]
    convert_element_type x6 -> x0, local copies, waits for them, and re-layouts: 4.83 us -> none  [score(): hidden = jax.nn.silu(pre).astype(jnp.bfloat16)]
  transfers between devices with their start and end apart: 8 -> 12, of which waited for: 3 -> 5; matrix products, arithmetic and copies ran while one was open for 2% -> 7% of each run, Pallas kernels for 0% -> 1%
where the time goes in v1:
time: 53.9 us; the launch traced here: 53.6 us
  starting transfers between devices  29.2 us (54%)
  waiting for transfers between devices  10.8 us (20%)
  Pallas kernels  8.81 us (16%)
  local copies, waits for them, and re-layouts  4.52 us (8%)
    ppermute x2, starting transfers between devices, exchange(): beside = lax.ppermute(field, 'tm', swap)  10.3 us
    ppermute x4, starting transfers between devices, summed(): lax.ppermute(value, 'tm', [(d, d ^ distance) for d in range(count)])  8.14 us
    ppermute x2, starting transfers between devices, exchange(): two = lax.ppermute(field, 'tm', far)  7.83 us
    ppermute x4, waiting for transfers between devices, summed(): lax.ppermute(value, 'tm', [(d, d ^ distance) for d in range(count)])  5.81 us
    ppermute x2, waiting for transfers between devices, exchange(): two = lax.ppermute(field, 'tm', far)  4.99 us
    pallas_call x1, Pallas kernels, on_device(): call(functools.partial(second_body, lon), [shape((rows, lon), f32), small...  3.23 us
    pallas_call x1, Pallas kernels, on_device(): call(functools.partial(first_body, lon), [shape((rows, width), f32), fiel...  3.09 us
    pallas_call x1, Pallas kernels, on_device(): pl.pallas_call(last_body, in_specs=[SMEM] + [VMEM] * 3, out_specs=VMEM, o...  1.6 us
  transfers between devices with their start and end apart: 12, of which 5 were waited for; matrix products, arithmetic and copies ran while one was open for 7% of the time, Pallas kernels for 1%

profile of v1, /device:TPU:0, one launch (start us, length us, event | category | flops | bytes accessed | tf_op | source)
XLA Modules:
  0.0 53.6 jit_solution(6901797391845740573)
XLA Ops:
  0.0 0.0 copy-start
  0.0 1.0 %copy-done = f32[1,64,1,1440]{3,2,1,0:T(1,128)S(1)} copy-done((f32[1,64,1,1440]{3,2,1,0:T(1,128)S(1)}, f32[1,64,1,1440]{3,2,1,0:T(1,128)}, u32[]{:S(2)}) %copy-start) | copy-done | bytes 368664
  1.0 0.0 copy-start.1
  1.0 0.0 copy-start.2
  1.0 0.0 copy-start.3
  1.0 0.0 copy-start.4
  1.0 0.1 shard_map.83.refs_2_
  1.1 0.8 %collective-permute-start.1 = (bf16[64,1536]{1,0:T(8,128)(2,1)S(1)}, bf16[64,1536]{1,0:T(8,128)(2,1)S(1)}, u32[]{:S(2)}, u32[]{:S(2)}) collective-permute-start(bf16[64,1536]{1,0:T(8,128)(2,1)S(1)} %shard_map.83.refs_2_), channel_id=1, source_target_pairs={{1,2},{3,4},{5,6},{7,8},{9,10},{11,12},{13,14},{2,1},{4,3},{6,5},{... | collective-permute-start | bytes 589832 | tf_op jit(solution)/shard_map/ppermute | solution.py:114
  2.0 4.4 %collective-permute-start.2 = (bf16[64,1536]{1,0:T(8,128)(2,1)S(1)}, bf16[64,1536]{1,0:T(8,128)(2,1)S(1)}, u32[]{:S(2)}, u32[]{:S(2)}) collective-permute-start(bf16[64,1536]{1,0:T(8,128)(2,1)S(1)} %shard_map.83.refs_2_), channel_id=1, source_target_pairs={{0,1},{1,0},{2,3},{3,2},{4,5},{5,4},{6,7},{7,6},{8,9},{9,8},{10,11... | collective-permute-start | bytes 589832 | tf_op jit(solution)/shard_map/ppermute | solution.py:116
  6.4 3.4 %collective-permute-start = (bf16[64,1536]{1,0:T(8,128)(2,1)S(1)}, bf16[64,1536]{1,0:T(8,128)(2,1)S(1)}, u32[]{:S(2)}, u32[]{:S(2)}) collective-permute-start(bf16[64,1536]{1,0:T(8,128)(2,1)S(1)} %shard_map.83.refs_2_), channel_id=1, source_target_pairs={{0,2},{2,4},{4,6},{6,8},{8,10},{10,12},{12,14},{3,1},{5,3},{7,5},{... | collective-permute-start | bytes 589832 | tf_op jit(solution)/shard_map/ppermute | solution.py:115
  9.8 0.0 collective-permute-done.1.refs_1_
  9.8 1.2 %collective-permute-start.3 = (bf16[64,1536]{1,0:T(8,128)(2,1)S(1)}, bf16[64,1536]{1,0:T(8,128)(2,1)S(1)}, u32[]{:S(2)}, u32[]{:S(2)}) collective-permute-start(bf16[64,1536]{1,0:T(8,128)(2,1)S(1)} %collective-permute-done.1.refs_1_), channel_id=1, source_target_pairs={{0,1},{1,0},{2,3},{3,2},{4,5},{5,4},{6,7},{7,6},{8,9},{9,8},{10,11... | collective-permute-start | bytes 589832 | tf_op jit(solution)/shard_map/ppermute | solution.py:117
  11.0 0.7 %copy.11.bias_ref.refs_8_ = f32[64,1]{1,0:T(8,128)S(1)} copy(f32[64,1]{0,1:T(1,128)} %bitcast.8) | data formatting | bytes 512 | tf_op jit(solution)/shard_map/broadcast_in_dim | solution.py:138
  11.7 0.9 %slice.9.refs_7_ = bf16[1,3,64,256]{3,2,1,0:T(8,128)(2,1)S(1)} slice(bf16[3,3,64,256]{3,2,1,0:T(8,128)(2,1)} %bitcast.6), slice={[1:2], [0:3], [0:64], [0:256]} | slice | bytes 196608 | tf_op jit(solution)/shard_map/slice | solution.py:137
  12.6 0.8 %copy.12.refs_6_ = f32[256,1]{1,0:T(8,128)S(1)} copy(f32[256,1]{0,1:T(1,128)} %bitcast.7) | data formatting | bytes 2048 | tf_op jit(solution)/shard_map/broadcast_in_dim | solution.py:138
  13.5 1.1 %slice.8.w_ref = bf16[1,3,320,256]{3,2,1,0:T(8,128)(2,1)S(1)} slice(bf16[3,3,320,256]{3,2,1,0:T(8,128)(2,1)} %bitcast.5), slice={[1:2], [0:3], [0:320], [0:256]} | slice | bytes 983040 | tf_op jit(solution)/shard_map/slice | solution.py:136
  14.5 0.0 copy-done.1
  14.5 0.0 copy-done.2
  14.6 0.0 copy-done.3
  14.6 0.0 copy-done.4
  14.6 0.8 %shard_map.82 = (f32[64,1536]{1,0:T(8,128)S(1)}, f32[1,128]{1,0:T(1,128)S(1)}, bf16[256,960]{1,0:T(8,128)(2,1)S(1)}) custom-call(s32[1]{0:T(128)} %bitcast.odd_ref, f32[1,64,1,1440]{3,2,1,0:T(1,128)S(1)} %copy-done.1, f32[1,64,1,1440]{3,2,1,0:T(1,128)S(1)} %copy-done.3, s32[1,64,1,1440]{3,2,1,0:T(1,128)S(1)} %copy-done.4, f32[1,64,1,1440]{3,2,1,0:T(1,128)S(1)} %copy-done.2, ...), custom_call_target="tpu_custom_call" | custom-call | tf_op jit(solution)/shard_map/pallas_call | solution.py:144
  15.3 0.0 collective-permute-done.2.refs_3_
  15.3 0.0 collective-permute-done.refs_0_
  15.4 0.0 collective-permute-done.3.refs_4_
  15.4 3.1 %shard_map.84 = (f32[64,1536]{1,0:T(8,128)S(1)}, bf16[64,1536]{1,0:T(8,128)(2,1)S(1)}) custom-call(bf16[64,1536]{1,0:T(8,128)(2,1)S(1)} %collective-permute-done.refs_0_, bf16[64,1536]{1,0:T(8,128)(2,1)S(1)} %collective-permute-done.1.refs_1_, bf16[64,1536]{1,0:T(8,128)(2,1)S(1)} %shard_map.83.refs_2_, bf16[64,1536]{1,0:T(8,128)(2,1)S(1)} %collective-permute-done.2.refs_3_, ...), custom_call_target="tpu_custom_call" | custom-call | tf_op jit(solution)/shard_map/pallas_call | solution.py:152
  18.5 0.7 %collective-permute-start.5 = (bf16[64,1536]{1,0:T(8,128)(2,1)S(1)}, bf16[64,1536]{1,0:T(8,128)(2,1)S(1)}, u32[]{:S(2)}, u32[]{:S(2)}) collective-permute-start(bf16[64,1536]{1,0:T(8,128)(2,1)S(1)} %get-tuple-element.15.refs_2_), channel_id=1, source_target_pairs={{1,2},{3,4},{5,6},{7,8},{9,10},{11,12},{13,14},{2,1},{4,3},{6,5},{... | collective-permute-start | bytes 589832 | tf_op jit(solution)/shard_map/ppermute | solution.py:114
  19.1 5.9 %collective-permute-start.6 = (bf16[64,1536]{1,0:T(8,128)(2,1)S(1)}, bf16[64,1536]{1,0:T(8,128)(2,1)S(1)}, u32[]{:S(2)}, u32[]{:S(2)}) collective-permute-start(bf16[64,1536]{1,0:T(8,128)(2,1)S(1)} %get-tuple-element.15.refs_2_), channel_id=1, source_target_pairs={{0,1},{1,0},{2,3},{3,2},{4,5},{5,4},{6,7},{7,6},{8,9},{9,8},{10,11... | collective-permute-start | bytes 589832 | tf_op jit(solution)/shard_map/ppermute | solution.py:116
  25.1 4.4 %collective-permute-start.4 = (bf16[64,1536]{1,0:T(8,128)(2,1)S(1)}, bf16[64,1536]{1,0:T(8,128)(2,1)S(1)}, u32[]{:S(2)}, u32[]{:S(2)}) collective-permute-start(bf16[64,1536]{1,0:T(8,128)(2,1)S(1)} %get-tuple-element.15.refs_2_), channel_id=1, source_target_pairs={{0,2},{2,4},{4,6},{6,8},{8,10},{10,12},{12,14},{3,1},{5,3},{7,5},{... | collective-permute-start | bytes 589832 | tf_op jit(solution)/shard_map/ppermute | solution.py:115
  29.5 0.0 collective-permute-done.5.refs_1_
  29.5 0.2 collective-permute-start.7
  29.7 0.0 collective-permute-done.6.refs_3_
  29.7 5.0 %collective-permute-done.4.refs_0_ = bf16[64,1536]{1,0:T(8,128)(2,1)S(1)} collective-permute-done((bf16[64,1536]{1,0:T(8,128)(2,1)S(1)}, bf16[64,1536]{1,0:T(8,128)(2,1)S(1)}, u32[]{:S(2)}, u32[]{:S(2)}) %collective-permute-start.4) | collective-permute-done | bytes 196640 | tf_op jit(solution)/shard_map/ppermute | solution.py:115
  34.7 0.0 collective-permute-done.7.refs_4_
  34.7 3.2 %shard_map.85 = (f32[64,1440]{1,0:T(8,128)S(1)}, f32[1,128]{1,0:T(1,128)S(1)}) custom-call(bf16[64,1536]{1,0:T(8,128)(2,1)S(1)} %collective-permute-done.4.refs_0_, bf16[64,1536]{1,0:T(8,128)(2,1)S(1)} %collective-permute-done.5.refs_1_, bf16[64,1536]{1,0:T(8,128)(2,1)S(1)} %get-tuple-element.15.refs_2_, ...), custom_call_target="tpu_custom_call" | custom-call | tf_op jit(solution)/shard_map/pallas_call | solution.py:155
  38.0 0.1 collective-permute-start.8
  38.0 1.1 %collective-permute-done.8 = f32[2,128]{1,0:T(2,128)S(1)} collective-permute-done((f32[2,128]{1,0:T(2,128)S(1)}, f32[2,128]{1,0:T(2,128)S(1)}, u32[]{:S(2)}, u32[]{:S(2)}) %collective-permute-start.8) | collective-permute-done | bytes 1056 | tf_op jit(solution)/shard_map/ppermute | solution.py:124
  39.2 2.5 %collective-permute-start.9 = (f32[2,128]{1,0:T(2,128)S(1)}, f32[2,128]{1,0:T(2,128)S(1)}, u32[]{:S(2)}, u32[]{:S(2)}) collective-permute-start(f32[2,128]{1,0:T(2,128)S(1)} %fusion), channel_id=1, source_target_pairs={{0,2},{1,3},{2,0},{3,1},{4,6},{5,7},{6,4},{7,5},{8,10},{9,11},{10,... | collective-permute-start | bytes 3080 | tf_op jit(solution)/shard_map/ppermute | solution.py:124
  41.8 1.6 %collective-permute-done.9 = f32[2,128]{1,0:T(2,128)S(1)} collective-permute-done((f32[2,128]{1,0:T(2,128)S(1)}, f32[2,128]{1,0:T(2,128)S(1)}, u32[]{:S(2)}, u32[]{:S(2)}) %collective-permute-start.9) | collective-permute-done | bytes 1056 | tf_op jit(solution)/shard_map/ppermute | solution.py:124
  43.3 2.5 %collective-permute-start.10 = (f32[2,128]{1,0:T(2,128)S(1)}, f32[2,128]{1,0:T(2,128)S(1)}, u32[]{:S(2)}, u32[]{:S(2)}) collective-permute-start(f32[2,128]{1,0:T(2,128)S(1)} %fusion.1), channel_id=1, source_target_pairs={{0,4},{1,5},{2,6},{3,7},{4,0},{5,1},{6,2},{7,3},{8,12},{9,13},{10,... | collective-permute-start | bytes 3080 | tf_op jit(solution)/shard_map/ppermute | solution.py:124
  45.8 1.6 %collective-permute-done.10 = f32[2,128]{1,0:T(2,128)S(1)} collective-permute-done((f32[2,128]{1,0:T(2,128)S(1)}, f32[2,128]{1,0:T(2,128)S(1)}, u32[]{:S(2)}, u32[]{:S(2)}) %collective-permute-start.10) | collective-permute-done | bytes 1056 | tf_op jit(solution)/shard_map/ppermute | solution.py:124
  47.4 3.0 %collective-permute-start.11 = (f32[2,128]{1,0:T(2,128)S(1)}, f32[2,128]{1,0:T(2,128)S(1)}, u32[]{:S(2)}, u32[]{:S(2)}) collective-permute-start(f32[2,128]{1,0:T(2,128)S(1)} %add.19), channel_id=1, source_target_pairs={{0,8},{1,9},{2,10},{3,11},{4,12},{5,13},{6,14},{7,15},{8,0},{9,1},... | collective-permute-start | bytes 3080 | tf_op jit(solution)/shard_map/ppermute | solution.py:124
  50.4 1.6 %collective-permute-done.11 = f32[2,128]{1,0:T(2,128)S(1)} collective-permute-done((f32[2,128]{1,0:T(2,128)S(1)}, f32[2,128]{1,0:T(2,128)S(1)}, u32[]{:S(2)}, u32[]{:S(2)}) %collective-permute-start.11) | collective-permute-done | bytes 1056 | tf_op jit(solution)/shard_map/ppermute | solution.py:124
  52.0 1.6 %shard_map.86 = f32[1,64,1,1440]{3,2,1,0:T(1,128)} custom-call(f32[2,128]{1,0:T(2,128)S(1)} %add.20.sums_ref, f32[64,1536]{1,0:T(8,128)S(1)} %get-tuple-element.16.refs_9_.predicted, f32[64,1440]{1,0:T(8,128)S(1)} %get-tuple-element.18.drift, f32[1,64,1,1440]{3,2,1,0:T(1,128)S(1)} %copy-done.2), custom_call_target="tpu_custom_call" | custom-call | tf_op jit(solution)/shard_map/pallas_call | solution.py:159
  (5 shorter events, 0.0 us)
Async XLA Ops:
  0.0 1.0 %copy-start = (f32[1,64,1,1440]{3,2,1,0:T(1,128)S(1)}, f32[1,64,1,1440]{3,2,1,0:T(1,128)}, u32[]{:S(2)}) copy-start(f32[1,64,1,1440]{3,2,1,0:T(1,128)} %state_ref.3) | copy-start | bytes 1105924
  1.0 13.5 %copy-start.1 = (f32[1,64,1,1440]{3,2,1,0:T(1,128)S(1)}, f32[1,64,1,1440]{3,2,1,0:T(1,128)}, u32[]{:S(2)}) copy-start(f32[1,64,1,1440]{3,2,1,0:T(1,128)} %state_ref.3) | copy-start | bytes 1105924
  1.0 13.5 %copy-start.2 = (f32[1,64,1,1440]{3,2,1,0:T(1,128)S(1)}, f32[1,64,1,1440]{3,2,1,0:T(1,128)}, u32[]{:S(2)}) copy-start(f32[1,64,1,1440]{3,2,1,0:T(1,128)} %noise_ref.3) | copy-start | bytes 1105924
  1.0 13.6 %copy-start.3 = (f32[1,64,1,1440]{3,2,1,0:T(1,128)S(1)}, f32[1,64,1,1440]{3,2,1,0:T(1,128)}, u32[]{:S(2)}) copy-start(f32[1,64,1,1440]{3,2,1,0:T(1,128)} %refs_10_.1) | copy-start | bytes 1105924
  1.0 13.6 %copy-start.4 = (s32[1,64,1,1440]{3,2,1,0:T(1,128)S(1)}, s32[1,64,1,1440]{3,2,1,0:T(1,128)}, u32[]{:S(2)}) copy-start(s32[1,64,1,1440]{3,2,1,0:T(1,128)} %refs_11_.1) | copy-start | bytes 1105924
  1.1 8.7 %collective-permute-start.1 = (bf16[64,1536]{1,0:T(8,128)(2,1)S(1)}, bf16[64,1536]{1,0:T(8,128)(2,1)S(1)}, u32[]{:S(2)}, u32[]{:S(2)}) collective-permute-start(bf16[64,1536]{1,0:T(8,128)(2,1)S(1)} %shard_map.83.refs_2_), channel_id=1, source_target_pairs={{1,2},{3,4},{5,6},{7,8},{9,10},{11,12},{13,14},{2,1},{4,3},{6,5},{... | collective-permute-start | bytes 589832 | tf_op jit(solution)/shard_map/ppermute | solution.py:114
  2.0 13.4 %collective-permute-start.2 = (bf16[64,1536]{1,0:T(8,128)(2,1)S(1)}, bf16[64,1536]{1,0:T(8,128)(2,1)S(1)}, u32[]{:S(2)}, u32[]{:S(2)}) collective-permute-start(bf16[64,1536]{1,0:T(8,128)(2,1)S(1)} %shard_map.83.refs_2_), channel_id=1, source_target_pairs={{0,1},{1,0},{2,3},{3,2},{4,5},{5,4},{6,7},{7,6},{8,9},{9,8},{10,11... | collective-permute-start | bytes 589832 | tf_op jit(solution)/shard_map/ppermute | solution.py:116
  6.4 9.0 %collective-permute-start = (bf16[64,1536]{1,0:T(8,128)(2,1)S(1)}, bf16[64,1536]{1,0:T(8,128)(2,1)S(1)}, u32[]{:S(2)}, u32[]{:S(2)}) collective-permute-start(bf16[64,1536]{1,0:T(8,128)(2,1)S(1)} %shard_map.83.refs_2_), channel_id=1, source_target_pairs={{0,2},{2,4},{4,6},{6,8},{8,10},{10,12},{12,14},{3,1},{5,3},{7,5},{... | collective-permute-start | bytes 589832 | tf_op jit(solution)/shard_map/ppermute | solution.py:115
  9.8 5.6 %collective-permute-start.3 = (bf16[64,1536]{1,0:T(8,128)(2,1)S(1)}, bf16[64,1536]{1,0:T(8,128)(2,1)S(1)}, u32[]{:S(2)}, u32[]{:S(2)}) collective-permute-start(bf16[64,1536]{1,0:T(8,128)(2,1)S(1)} %collective-permute-done.1.refs_1_), channel_id=1, source_target_pairs={{0,1},{1,0},{2,3},{3,2},{4,5},{5,4},{6,7},{7,6},{8,9},{9,8},{10,11... | collective-permute-start | bytes 589832 | tf_op jit(solution)/shard_map/ppermute | solution.py:117
  18.5 11.0 %collective-permute-start.5 = (bf16[64,1536]{1,0:T(8,128)(2,1)S(1)}, bf16[64,1536]{1,0:T(8,128)(2,1)S(1)}, u32[]{:S(2)}, u32[]{:S(2)}) collective-permute-start(bf16[64,1536]{1,0:T(8,128)(2,1)S(1)} %get-tuple-element.15.refs_2_), channel_id=1, source_target_pairs={{1,2},{3,4},{5,6},{7,8},{9,10},{11,12},{13,14},{2,1},{4,3},{6,5},{... | collective-permute-start | bytes 589832 | tf_op jit(solution)/shard_map/ppermute | solution.py:114
  19.1 10.6 %collective-permute-start.6 = (bf16[64,1536]{1,0:T(8,128)(2,1)S(1)}, bf16[64,1536]{1,0:T(8,128)(2,1)S(1)}, u32[]{:S(2)}, u32[]{:S(2)}) collective-permute-start(bf16[64,1536]{1,0:T(8,128)(2,1)S(1)} %get-tuple-element.15.refs_2_), channel_id=1, source_target_pairs={{0,1},{1,0},{2,3},{3,2},{4,5},{5,4},{6,7},{7,6},{8,9},{9,8},{10,11... | collective-permute-start | bytes 589832 | tf_op jit(solution)/shard_map/ppermute | solution.py:116
  25.1 9.6 %collective-permute-start.4 = (bf16[64,1536]{1,0:T(8,128)(2,1)S(1)}, bf16[64,1536]{1,0:T(8,128)(2,1)S(1)}, u32[]{:S(2)}, u32[]{:S(2)}) collective-permute-start(bf16[64,1536]{1,0:T(8,128)(2,1)S(1)} %get-tuple-element.15.refs_2_), channel_id=1, source_target_pairs={{0,2},{2,4},{4,6},{6,8},{8,10},{10,12},{12,14},{3,1},{5,3},{7,5},{... | collective-permute-start | bytes 589832 | tf_op jit(solution)/shard_map/ppermute | solution.py:115
  29.5 5.2 %collective-permute-start.7 = (bf16[64,1536]{1,0:T(8,128)(2,1)S(1)}, bf16[64,1536]{1,0:T(8,128)(2,1)S(1)}, u32[]{:S(2)}, u32[]{:S(2)}) collective-permute-start(bf16[64,1536]{1,0:T(8,128)(2,1)S(1)} %collective-permute-done.5.refs_1_), channel_id=1, source_target_pairs={{0,1},{1,0},{2,3},{3,2},{4,5},{5,4},{6,7},{7,6},{8,9},{9,8},{10,11... | collective-permute-start | bytes 589832 | tf_op jit(solution)/shard_map/ppermute | solution.py:117
  38.0 1.2 %collective-permute-start.8 = (f32[2,128]{1,0:T(2,128)S(1)}, f32[2,128]{1,0:T(2,128)S(1)}, u32[]{:S(2)}, u32[]{:S(2)}) collective-permute-start(f32[2,128]{1,0:T(2,128)S(1)} %pad_maximum_fusion), channel_id=1, source_target_pairs={{0,1},{1,0},{2,3},{3,2},{4,5},{5,4},{6,7},{7,6},{8,9},{9,8},{10,11... | collective-permute-start | bytes 3080 | tf_op jit(solution)/shard_map/ppermute | solution.py:124
  39.2 4.1 %collective-permute-start.9 = (f32[2,128]{1,0:T(2,128)S(1)}, f32[2,128]{1,0:T(2,128)S(1)}, u32[]{:S(2)}, u32[]{:S(2)}) collective-permute-start(f32[2,128]{1,0:T(2,128)S(1)} %fusion), channel_id=1, source_target_pairs={{0,2},{1,3},{2,0},{3,1},{4,6},{5,7},{6,4},{7,5},{8,10},{9,11},{10,... | collective-permute-start | bytes 3080 | tf_op jit(solution)/shard_map/ppermute | solution.py:124
  43.3 4.0 %collective-permute-start.10 = (f32[2,128]{1,0:T(2,128)S(1)}, f32[2,128]{1,0:T(2,128)S(1)}, u32[]{:S(2)}, u32[]{:S(2)}) collective-permute-start(f32[2,128]{1,0:T(2,128)S(1)} %fusion.1), channel_id=1, source_target_pairs={{0,4},{1,5},{2,6},{3,7},{4,0},{5,1},{6,2},{7,3},{8,12},{9,13},{10,... | collective-permute-start | bytes 3080 | tf_op jit(solution)/shard_map/ppermute | solution.py:124
  47.4 4.6 %collective-permute-start.11 = (f32[2,128]{1,0:T(2,128)S(1)}, f32[2,128]{1,0:T(2,128)S(1)}, u32[]{:S(2)}, u32[]{:S(2)}) collective-permute-start(f32[2,128]{1,0:T(2,128)S(1)} %add.19), channel_id=1, source_target_pairs={{0,8},{1,9},{2,10},{3,11},{4,12},{5,13},{6,14},{7,15},{8,0},{9,1},... | collective-permute-start | bytes 3080 | tf_op jit(solution)/shard_map/ppermute | solution.py:124
